TPU v7x, 512 devices: a whole 4x4x16 slice. The times are simulated.
512 devices in a mesh: lead: 4 (over x_hi, core), lat: 32 (over x_lo, z), lon: 4 (over y).
Axes of the slice: x: 4 (x_hi: 2, x_lo: 2; x = x_hi * 2 + x_lo), y: 4, z: 16, core: 2. Of those that a mesh axis runs over, the one named last changes fastest.
Arguments:
- head_grads: bfloat16 [8, 8, 128, 128, 128], P('lead', None, 'lat', 'lon'), may hold values from -6 to 6
- head_weights: bfloat16 [8, 9, 256, 128], P('lead'), may hold values from -0.0625 to 0.0625
- encoder_input: bfloat16 [8, 128, 128, 128], P('lead', 'lat', 'lon'), may hold values from -6 to 6
- pre_first: bfloat16 [8, 128, 128, 256], P('lead', 'lat', 'lon'), may hold values from -8 to 8
- pre_second: bfloat16 [8, 128, 128, 256], P('lead', 'lat', 'lon'), may hold values from -8 to 8
- w_first: bfloat16 [9, 128, 256], replicated, may hold values from -0.1875 to 0.1875
- w_second: bfloat16 [9, 256, 256], replicated, may hold values from -0.125 to 0.125
Outputs:
- input_grad: bfloat16 [8, 128, 128, 128], P('lead', 'lat', 'lon')
- weight_grad_first: float32 [294912], P(('lat', 'lon'))
- weight_grad_second: float32 [589824], P(('lat', 'lon'))
All inputs are finite; a program needn't handle non-finite values.
Results may differ from a plain program's by a relative error of at most 0.022.
Values may be sent and summed in bfloat16 or wider, within the bound.
A program may use at most 64 MiB of HBM per device.

v0:
```python
import math
import jax
import jax.numpy as jnp
from jax import lax
from jax.sharding import PartitionSpec as P

OFFSETS = [(-1, -1), (-1, 0), (-1, 1), (0, -1), (0, 0), (0, 1), (1, -1), (1, 0), (1, 1)]


def with_halo(block, sides, width, periodic):
    for axis, dim in sides:
        count = lax.axis_size(axis)
        forward = [(i, i + 1) for i in range(count - 1)]
        if periodic:
            forward.append((count - 1, 0))
        backward = [(target, source) for source, target in forward]
        low = lax.ppermute(
            lax.slice_in_dim(block, block.shape[dim] - width, None, axis=dim), axis, forward
        )
        high = lax.ppermute(lax.slice_in_dim(block, 0, width, axis=dim), axis, backward)
        block = jnp.concatenate([low, block, high], axis=dim)
    return block


def gelu_value(values):
    return 0.5 * values * (1.0 + lax.erf(values * 0.7071067811865476))


def gelu_slope(values):
    return (
        0.5 * (1.0 + lax.erf(values * 0.7071067811865476))
        + values * jnp.exp(-0.5 * values * values) * 0.3989422804014327
    )


def widen(source):
    extended = with_halo(source, (("lon", 2),), 1, True)
    return with_halo(extended, (("lat", 1),), 1, False)


def window(padded, step_row, step_col):
    height = padded.shape[-3] - 2
    breadth = padded.shape[-2] - 2
    return padded[
        ..., 1 + step_row : 1 + step_row + height, 1 + step_col : 1 + step_col + breadth, :
    ]


def per_device(head_grads, head_weights, encoder_input, pre_first, pre_second, w_first, w_second):
    heads_here, batch_all, height, breadth, head_channels = head_grads.shape
    samples = encoder_input.shape[0]
    latent_width = head_weights.shape[2]
    merged = head_grads.reshape(heads_here * batch_all, height, breadth, head_channels)
    padded_heads = widen(merged).reshape(
        heads_here, batch_all, height + 2, breadth + 2, head_channels
    )
    summed = jnp.zeros(
        (samples * lax.axis_size("lead"), height, breadth, latent_width), jnp.float32
    )
    for latent_offset, (latent_step_row, latent_step_col) in enumerate(OFFSETS):
        moved = window(padded_heads, -latent_step_row, -latent_step_col)
        summed = summed + jnp.einsum(
            "hbrcj,hdj->brcd",
            moved,
            head_weights[:, latent_offset],
            preferred_element_type=jnp.float32,
        )
    latent_grad = lax.psum_scatter(
        summed.astype(jnp.bfloat16), "lead", scatter_dimension=0, tiled=True
    ).astype(jnp.float32)
    pre_two = pre_second.astype(jnp.float32)
    pre_one = pre_first.astype(jnp.float32)
    da_second = (latent_grad * gelu_slope(pre_two)).astype(jnp.bfloat16)
    act_first = gelu_value(pre_one).astype(jnp.bfloat16)
    padded_act = widen(act_first)
    padded_input = widen(encoder_input)
    padded_second = widen(da_second)
    grad_second = []
    linear_first = jnp.zeros((samples, height, breadth, latent_width), jnp.float32)
    for offset, (step_row, step_col) in enumerate(OFFSETS):
        grad_second.append(
            jnp.einsum(
                "brci,brcd->id",
                window(padded_act, step_row, step_col),
                da_second,
                preferred_element_type=jnp.float32,
            )
        )
        linear_first = linear_first + jnp.einsum(
            "brcd,id->brci",
            window(padded_second, -step_row, -step_col),
            w_second[offset],
            preferred_element_type=jnp.float32,
        )
    da_first = (linear_first * gelu_slope(pre_one)).astype(jnp.bfloat16)
    padded_first = widen(da_first)
    grad_first = []
    input_sum = jnp.zeros((samples, height, breadth, w_first.shape[1]), jnp.float32)
    for offset, (step_row, step_col) in enumerate(OFFSETS):
        grad_first.append(
            jnp.einsum(
                "brcj,brcd->jd",
                window(padded_input, step_row, step_col),
                da_first,
                preferred_element_type=jnp.float32,
            )
        )
        input_sum = input_sum + jnp.einsum(
            "brcd,jd->brcj",
            window(padded_first, -step_row, -step_col),
            w_first[offset],
            preferred_element_type=jnp.float32,
        )
    input_grad = input_sum.astype(jnp.bfloat16)
    cells_total = (
        samples
        * lax.axis_size("lead")
        * height
        * lax.axis_size("lat")
        * breadth
        * lax.axis_size("lon")
    )
    norm_factor = 1.0 / math.sqrt(cells_total)
    flat_first = (jnp.stack(grad_first) * norm_factor).reshape(-1)
    flat_second = (jnp.stack(grad_second) * norm_factor).reshape(-1)
    whole_first, whole_second = (
        lax.psum(flat_first.astype(jnp.bfloat16), "lead").astype(jnp.float32),
        lax.psum(flat_second.astype(jnp.bfloat16), "lead").astype(jnp.float32),
    )
    result_first, result_second = (
        lax.psum_scatter(whole_first, ("lat", "lon"), scatter_dimension=0, tiled=True),
        lax.psum_scatter(whole_second, ("lat", "lon"), scatter_dimension=0, tiled=True),
    )
    return (input_grad, result_first, result_second)


def solution(mesh):
    in_specs = (
        P("lead", None, "lat", "lon", None),
        P("lead", None, None, None),
        P("lead", "lat", "lon", None),
        P("lead", "lat", "lon", None),
        P("lead", "lat", "lon", None),
        P(),
        P(),
    )
    out_specs = (P("lead", "lat", "lon", None), P(("lat", "lon")), P(("lat", "lon")))
    return jax.shard_map(
        per_device, mesh=mesh, in_specs=in_specs, out_specs=out_specs, check_vma=False
    )
```

profile of v0, /device:TPU:2, one launch (start us, length us, event | category | flops | bytes accessed | tf_op | source)
XLA Modules:
  0.0 843.0 jit_solution(9377522992387471817)
XLA Ops:
  8.6 3.5 collective-permute-start
  12.1 3.6 collective-permute-start.1
  15.7 2.0 collective-permute-done.1
  17.8 3.8 collective-permute-start.2
  21.6 9.5 %collective-permute-start.3 = (bf16[16,1,34,128]{3,0,2,1:T(8,128)(2,1)S(1)}, bf16[16,1,34,128]{3,0,2,1:T(8,128)(2,1)S(1)}, u32[]{:S(2)}, u32[]{:S(2)}) collective-permute-start(bf16[16,1,34,128]{3,0,2,1:T(8,128)(2,1)S(1)} %get-tuple-element.17), channel_id=1, source_target_pairs={{4,0},{8,4},{12,8},{16,12},{20,16},{24,20},{28,24},{32,28},{36,32}... | collective-permute-start | bytes 417800 | tf_op jit(solution)/shard_map/ppermute | solution.py:20
  39.5 3.5 collective-permute-start.12
  43.0 3.6 collective-permute-start.13
  46.7 2.3 collective-permute-start.16
  49.0 4.8 collective-permute-start.17
  58.3 6.5 collective-permute-start.15
  66.8 6.0 collective-permute-start.19
  74.5 7.0 reduce-scatter.2.cloned.1.call-done
  85.1 4.8 collective-permute-start.5
  92.0 2.2 copy.134
  94.3 2.4 collective-permute-done.4
  96.7 6.8 collective-permute-start.6
  105.7 5.8 collective-permute-done.7
  115.3 2.8 collective-permute-start.9
  118.1 3.1 collective-permute-start.8
  122.7 2.1 collective-permute-done.8
  126.8 3.9 collective-permute-start.11
  130.9 4.0 collective-permute-done.11
  137.0 48.8 %all-reduce.7.cloned.1.call-done = (bf16[294912]{0:T(1024)(128)(2,1)}, bf16[589824]{0:T(1024)(128)(2,1)}) async-done(((bf16[294912]{0:T(1024)(128)(2,1)}, bf16[589824]{0:T(1024)(128)(2,1)}), (bf16[294912]{0:T(1024)(128)(2,1)}, bf16[589824]{0:T(1024)(128)(2,1)})) %all-reduce.7.cloned.1.call-update) | async-done | bytes 1769488 | tf_op jit(solution)/shard_map/psum | solution.py:127
  185.7 649.0 %all-reduce.8 = (f32[294912]{0:T(1024)S(1)}, f32[589824]{0:T(1024)S(1)}) all-reduce(bf16[294912]{0:T(1024)(128)(2,1)} %get-tuple-element.5, bf16[589824]{0:T(1024)(128)(2,1)} %get-tuple-element.6), channel_id=3, replica_groups=mesh['lead'=4,'lat'=32,'lon'=4] {'lat','lon'}, use_global_device_ids=true, to_apply=%region_2.0.clone | all-reduce | flops 884736 | bytes 5308416
  (106 shorter events, 35.2 us)
Async XLA Ops:
  7.2 74.4 %reduce-scatter.2.cloned.1.call-start = ((), (), s32[]{:S(2)}) async-start(), calls=%async_computation.1 | async-start | bytes 655360 | tf_op jit(solution)/shard_map/reduce_scatter | solution.py:68
  8.6 7.1 collective-permute-start
  12.1 5.6 collective-permute-start.1
  17.8 14.4 %collective-permute-start.2 = (bf16[16,1,34,128]{3,0,2,1:T(8,128)(2,1)S(1)}, bf16[16,1,34,128]{3,0,2,1:T(8,128)(2,1)S(1)}, u32[]{:S(2)}, u32[]{:S(2)}) collective-permute-start(bf16[16,1,34,128]{3,0,2,1:T(8,128)(2,1)S(1)} %get-tuple-element.16), channel_id=1, source_target_pairs={{0,4},{4,8},{8,12},{12,16},{16,20},{20,24},{24,28},{28,32},{32,36}... | collective-permute-start | bytes 417800 | tf_op jit(solution)/shard_map/ppermute | solution.py:17
  21.6 12.1 %collective-permute-start.3 = (bf16[16,1,34,128]{3,0,2,1:T(8,128)(2,1)S(1)}, bf16[16,1,34,128]{3,0,2,1:T(8,128)(2,1)S(1)}, u32[]{:S(2)}, u32[]{:S(2)}) collective-permute-start(bf16[16,1,34,128]{3,0,2,1:T(8,128)(2,1)S(1)} %get-tuple-element.17), channel_id=1, source_target_pairs={{4,0},{8,4},{12,8},{16,12},{20,16},{24,20},{28,24},{32,28},{36,32}... | collective-permute-start | bytes 417800 | tf_op jit(solution)/shard_map/ppermute | solution.py:20
  37.9 8.6 %copy-start.3 = (bf16[2,4,32,256]{3,2,1,0:T(8,128)(2,1)S(1)}, bf16[2,4,32,256]{3,2,1,0:T(8,128)(2,1)}, u32[]{:S(2)}) copy-start(bf16[2,4,32,256]{3,2,1,0:T(8,128)(2,1)} %param.10) | copy-start | bytes 393220
  39.4 42.2 %copy-start.5 = (bf16[2,4,32,256]{3,2,1,0:T(8,128)(2,1)S(1)}, bf16[2,4,32,256]{3,2,1,0:T(8,128)(2,1)}, u32[]{:S(2)}) copy-start(bf16[2,4,32,256]{3,2,1,0:T(8,128)(2,1)} %param.11) | copy-start | bytes 393220
  39.4 146.3 %all-reduce.7.cloned.1.call-start = ((), (), s32[]{:S(2)}) async-start(), calls=%async_computation.2 | async-start | bytes 3538944 | tf_op jit(solution)/shard_map/psum | solution.py:127
  39.5 16.8 %collective-permute-start.12 = (bf16[2,4,1,128]{3,2,1,0:T(2,128)(2,1)S(1)}, bf16[2,4,1,128]{3,2,1,0:T(2,128)(2,1)S(1)}, u32[]{:S(2)}, u32[]{:S(2)}) collective-permute-start(bf16[2,4,1,128]{3,2,1,0:T(2,128)(2,1)S(1)} %get-tuple-element.42), channel_id=1, source_target_pairs={{0,1},{1,2},{2,3},{3,0},{4,5},{5,6},{6,7},{7,4},{8,9},{9,10},{10,1... | collective-permute-start | bytes 6152 | tf_op jit(solution)/shard_map/ppermute | solution.py:17
  43.0 13.3 %collective-permute-start.13 = (bf16[2,4,1,128]{3,2,1,0:T(2,128)(2,1)S(1)}, bf16[2,4,1,128]{3,2,1,0:T(2,128)(2,1)S(1)}, u32[]{:S(2)}, u32[]{:S(2)}) collective-permute-start(bf16[2,4,1,128]{3,2,1,0:T(2,128)(2,1)S(1)} %get-tuple-element.43), channel_id=1, source_target_pairs={{1,0},{2,1},{3,2},{0,3},{5,4},{6,5},{7,6},{4,7},{9,8},{10,9},{11,1... | collective-permute-start | bytes 6152 | tf_op jit(solution)/shard_map/ppermute | solution.py:20
  46.7 18.1 %collective-permute-start.16 = (bf16[2,4,1,256]{3,2,1,0:T(2,128)(2,1)S(1)}, bf16[2,4,1,256]{3,2,1,0:T(2,128)(2,1)S(1)}, u32[]{:S(2)}, u32[]{:S(2)}) collective-permute-start(bf16[2,4,1,256]{3,2,1,0:T(2,128)(2,1)S(1)} %get-tuple-element.32), channel_id=1, source_target_pairs={{0,1},{1,2},{2,3},{3,0},{4,5},{5,6},{6,7},{7,4},{8,9},{9,10},{10,1... | collective-permute-start | bytes 12296 | tf_op jit(solution)/shard_map/ppermute | solution.py:17
  49.0 15.8 %collective-permute-start.17 = (bf16[2,4,1,256]{3,2,1,0:T(2,128)(2,1)S(1)}, bf16[2,4,1,256]{3,2,1,0:T(2,128)(2,1)S(1)}, u32[]{:S(2)}, u32[]{:S(2)}) collective-permute-start(bf16[2,4,1,256]{3,2,1,0:T(2,128)(2,1)S(1)} %get-tuple-element.33), channel_id=1, source_target_pairs={{1,0},{2,1},{3,2},{0,3},{5,4},{6,5},{7,6},{4,7},{9,8},{10,9},{11,1... | collective-permute-start | bytes 12296 | tf_op jit(solution)/shard_map/ppermute | solution.py:20
  56.4 16.4 %collective-permute-start.14 = (bf16[2,1,34,128]{3,2,1,0:T(8,128)(2,1)S(1)}, bf16[2,1,34,128]{3,2,1,0:T(8,128)(2,1)S(1)}, u32[]{:S(2)}, u32[]{:S(2)}) collective-permute-start(bf16[2,1,34,128]{3,2,1,0:T(8,128)(2,1)S(1)} %get-tuple-element.41), channel_id=1, source_target_pairs={{0,4},{4,8},{8,12},{12,16},{16,20},{20,24},{24,28},{28,32},{32,36}... | collective-permute-start | bytes 52232 | tf_op jit(solution)/shard_map/ppermute | solution.py:17
  58.3 14.5 %collective-permute-start.15 = (bf16[2,1,34,128]{3,2,1,0:T(8,128)(2,1)S(1)}, bf16[2,1,34,128]{3,2,1,0:T(8,128)(2,1)S(1)}, u32[]{:S(2)}, u32[]{:S(2)}) collective-permute-start(bf16[2,1,34,128]{3,2,1,0:T(8,128)(2,1)S(1)} %get-tuple-element.40), channel_id=1, source_target_pairs={{4,0},{8,4},{12,8},{16,12},{20,16},{24,20},{28,24},{32,28},{36,32}... | collective-permute-start | bytes 52232 | tf_op jit(solution)/shard_map/ppermute | solution.py:20
  64.8 8.1 collective-permute-start.18
  66.8 7.7 collective-permute-start.19
  85.1 9.2 %collective-permute-start.5 = (bf16[2,4,1,256]{3,2,1,0:T(2,128)(2,1)S(1)}, bf16[2,4,1,256]{3,2,1,0:T(2,128)(2,1)S(1)}, u32[]{:S(2)}, u32[]{:S(2)}) collective-permute-start(bf16[2,4,1,256]{3,2,1,0:T(2,128)(2,1)S(1)} %get-tuple-element.37), channel_id=1, source_target_pairs={{1,0},{2,1},{3,2},{0,3},{5,4},{6,5},{7,6},{4,7},{9,8},{10,9},{11,1... | collective-permute-start | bytes 12296 | tf_op jit(solution)/shard_map/ppermute | solution.py:20
  89.9 6.8 collective-permute-start.4
  96.7 9.0 %collective-permute-start.6 = (bf16[2,1,34,256]{3,2,1,0:T(8,128)(2,1)S(1)}, bf16[2,1,34,256]{3,2,1,0:T(8,128)(2,1)S(1)}, u32[]{:S(2)}, u32[]{:S(2)}) collective-permute-start(bf16[2,1,34,256]{3,2,1,0:T(8,128)(2,1)S(1)} %get-tuple-element.30), channel_id=1, source_target_pairs={{4,0},{8,4},{12,8},{16,12},{20,16},{24,20},{28,24},{32,28},{36,32}... | collective-permute-start | bytes 104456 | tf_op jit(solution)/shard_map/ppermute | solution.py:20
  103.5 8.0 collective-permute-start.7
  115.3 7.4 collective-permute-start.9
  118.1 6.8 collective-permute-start.8
  124.9 6.0 collective-permute-start.10
  126.8 8.1 collective-permute-start.11
  (4 other events, 16.3 us)
Sparse Core Ops, SparseCore 0:
  39.5 41.9 reduce-scatter.1
  122.8 62.8 all-reduce.6
where the time goes:
time: 844 us; the launch traced here: 843 us
  blocking collectives  649 us (77%)
  starting transfers between devices  78 us (9%)
  waiting for transfers between devices  76.3 us (9%)
  between operations  16.1 us (2%)
  matrix products  12.5 us (1%)
  local copies, waits for them, and re-layouts  8.96 us (1%)
    unnamed x1, blocking collectives  649 us
    ppermute x10, starting transfers between devices, with_halo(): lax.ppermute(lax.slice_in_dim(block, 0, width, axis=dim), axis, backward)  50.2 us
    psum x1, waiting for transfers between devices, per_device(): lax.psum(flat_first.astype(jnp.bfloat16), 'lead').astype(jnp.float32)  48.8 us
    ppermute x10, starting transfers between devices, with_halo(): lax.ppermute(lax.slice_in_dim(block, block.shape[dim] - width, None, axis...  27.7 us
  transfers between devices with their start and end apart: 22, of which 10 were waited for; matrix products, arithmetic and copies ran while one was open for 1% of the time, Pallas kernels for 0%

commit v1 on v0

--- a/solution.py
+++ b/solution.py
@@ -124,7 +124,9 @@
     flat_first = (jnp.stack(grad_first) * norm_factor).reshape(-1)
     flat_second = (jnp.stack(grad_second) * norm_factor).reshape(-1)
     whole_first, whole_second = (
-        lax.psum(flat_first.astype(jnp.bfloat16), "lead").astype(jnp.float32),
+        jnp.sum(lax.all_gather(flat_first.astype(jnp.bfloat16), "lead"), axis=0).astype(
+            jnp.float32
+        ),
         lax.psum(flat_second.astype(jnp.bfloat16), "lead").astype(jnp.float32),
     )
     result_first, result_second = (

time: 844 us -> 871 us (1.032)
  waiting for transfers between devices: 76.3 us -> 90.7 us
  other arithmetic: 2.11 us -> 15.4 us
    all_gather x0 -> x1, waiting for transfers between devices: none -> 51.5 us  [per_device(): lax.all_gather(flat_first.astype(jnp.bfloat16), 'lead')]
    psum x1, waiting for transfers between devices: 48.8 us -> 6.41 us  [per_device(): lax.psum(flat_second.astype(jnp.bfloat16), 'lead').astype(jnp.float32)]
    reduce_sum x0 -> x1, other arithmetic: none -> 13.3 us  [per_device(): jnp.sum(lax.all_gather(flat_first.astype(jnp.bfloat16), 'lead'), axis=0)]
  transfers between devices with their start and end apart: 22 -> 23, of which waited for: 10 -> 11; matrix products, arithmetic and copies ran while one was open for 1% -> 1% of each run, Pallas kernels for 0% -> 0%
where the time goes in v1:
time: 871 us; the launch traced here: 870 us
  blocking collectives  648 us (74%)
  waiting for transfers between devices  90.7 us (10%)
  starting transfers between devices  78.2 us (9%)
  between operations  15.8 us (2%)
  other arithmetic  15.4 us (2%)
  matrix products  12.5 us (1%)
  local copies, waits for them, and re-layouts  9.67 us (1%)
    unnamed x1, blocking collectives  648 us
    all_gather x1, waiting for transfers between devices, per_device(): lax.all_gather(flat_first.astype(jnp.bfloat16), 'lead')  51.5 us
    ppermute x10, starting transfers between devices, with_halo(): lax.ppermute(lax.slice_in_dim(block, 0, width, axis=dim), axis, backward)  49.4 us
    ppermute x10, starting transfers between devices, with_halo(): lax.ppermute(lax.slice_in_dim(block, block.shape[dim] - width, None, axis...  28.8 us
    ppermute x10, waiting for transfers between devices, with_halo(): lax.ppermute(lax.slice_in_dim(block, block.shape[dim] - width, None, axis...  18.1 us
  transfers between devices with their start and end apart: 23, of which 11 were waited for; matrix products, arithmetic and copies ran while one was open for 1% of the time, Pallas kernels for 0%

profile of v1, /device:TPU:2, one launch (start us, length us, event | category | flops | bytes accessed | tf_op | source)
XLA Modules:
  0.0 870.4 jit_solution(6655406208567329598)
XLA Ops:
  8.6 3.5 collective-permute-start
  12.1 3.6 collective-permute-start.1
  17.8 3.8 collective-permute-start.2
  21.6 9.5 %collective-permute-start.3 = (bf16[16,1,34,128]{3,0,2,1:T(8,128)(2,1)S(1)}, bf16[16,1,34,128]{3,0,2,1:T(8,128)(2,1)S(1)}, u32[]{:S(2)}, u32[]{:S(2)}) collective-permute-start(bf16[16,1,34,128]{3,0,2,1:T(8,128)(2,1)S(1)} %get-tuple-element.15), channel_id=1, source_target_pairs={{4,0},{8,4},{12,8},{16,12},{20,16},{24,20},{28,24},{32,28},{36,32}... | collective-permute-start | bytes 417800 | tf_op jit(solution)/shard_map/ppermute | solution.py:20
  39.5 3.5 collective-permute-start.12
  43.0 3.6 collective-permute-start.13
  46.7 2.3 collective-permute-start.16
  49.0 4.8 collective-permute-start.17
  55.7 6.5 collective-permute-start.15
  64.2 6.0 collective-permute-start.19
  72.0 9.6 %reduce-scatter.2.cloned.1.call-done = bf16[2,4,32,256]{3,2,1,0:T(8,128)(2,1)} async-done(((bf16[8,4,32,256]{3,2,1,0:T(8,128)(2,1)}), bf16[2,4,32,256]{3,2,1,0:T(8,128)(2,1)}) %reduce-scatter.2.cloned.1.call-update) | async-done | bytes 131088 | tf_op jit(solution)/shard_map/reduce_scatter | solution.py:68
  85.1 2.2 copy.133
  87.4 4.8 collective-permute-start.5
  94.4 4.6 collective-permute-done.4
  99.0 6.8 collective-permute-start.6
  108.0 5.9 collective-permute-done.7
  123.6 3.9 collective-permute-start.8
  127.7 2.6 collective-permute-done.8
  132.3 4.1 collective-permute-start.11
  136.6 3.8 collective-permute-done.11
  142.5 6.4 all-reduce.6.cloned.1.call-done
  148.9 51.5 %all-gather.3.cloned.1.call-done = bf16[4,1,294912]{2,1,0:T(2,128)(2,1)} async-done(((bf16[1,1,294912]{2,1,0:T(2,128)(2,1)}), bf16[4,1,294912]{2,1,0:T(2,128)(2,1)}) %all-gather.3.cloned.1.call-update) | async-done | bytes 2359312 | tf_op jit(solution)/shard_map/all_gather | solution.py:127
  200.4 13.3 %reduce_sum.12 = bf16[294912]{0:T(1024)(128)(2,1)S(1)} reduce(bf16[4,1,294912]{2,1,0:T(2,128)(2,1)} %all-gather.3.cloned.1.call-done, bf16[]{:T(256)} %constant.6.clone.1), dimensions={0,1}, to_apply=%region_1.0 | reduce | flops 884736 | bytes 2949122 | tf_op jit(solution)/shard_map/reduce_sum | solution.py:127
  213.7 648.1 %all-reduce.7 = (f32[294912]{0:T(1024)S(1)}, f32[589824]{0:T(1024)}) all-reduce(bf16[294912]{0:T(1024)(128)(2,1)S(1)} %reduce_sum.12, bf16[589824]{0:T(1024)(128)(2,1)S(1)} %copy-done.1), channel_id=3, replica_groups=mesh['lead'=4,'lat'=32,'lon'=4] {'lat','lon'}, use_global_device_ids=true, to_apply=%region_2.0.clone | all-reduce | flops 884736 | bytes 5308416
  (112 shorter events, 39.9 us)
Async XLA Ops:
  7.2 74.5 %reduce-scatter.2.cloned.1.call-start = ((), (), s32[]{:S(2)}) async-start(), calls=%async_computation.1 | async-start | bytes 655360 | tf_op jit(solution)/shard_map/reduce_scatter | solution.py:68
  8.6 7.1 collective-permute-start
  12.1 5.6 collective-permute-start.1
  17.8 14.4 %collective-permute-start.2 = (bf16[16,1,34,128]{3,0,2,1:T(8,128)(2,1)S(1)}, bf16[16,1,34,128]{3,0,2,1:T(8,128)(2,1)S(1)}, u32[]{:S(2)}, u32[]{:S(2)}) collective-permute-start(bf16[16,1,34,128]{3,0,2,1:T(8,128)(2,1)S(1)} %get-tuple-element.14), channel_id=1, source_target_pairs={{0,4},{4,8},{8,12},{12,16},{16,20},{20,24},{24,28},{28,32},{32,36}... | collective-permute-start | bytes 417800 | tf_op jit(solution)/shard_map/ppermute | solution.py:17
  21.6 12.1 %collective-permute-start.3 = (bf16[16,1,34,128]{3,0,2,1:T(8,128)(2,1)S(1)}, bf16[16,1,34,128]{3,0,2,1:T(8,128)(2,1)S(1)}, u32[]{:S(2)}, u32[]{:S(2)}) collective-permute-start(bf16[16,1,34,128]{3,0,2,1:T(8,128)(2,1)S(1)} %get-tuple-element.15), channel_id=1, source_target_pairs={{4,0},{8,4},{12,8},{16,12},{20,16},{24,20},{28,24},{32,28},{36,32}... | collective-permute-start | bytes 417800 | tf_op jit(solution)/shard_map/ppermute | solution.py:20
  39.4 109.5 %all-reduce.6.cloned.1.call-start = ((), (), s32[]{:S(2)}) async-start(), calls=%async_computation.2 | async-start | bytes 2359296 | tf_op jit(solution)/shard_map/psum | solution.py:130
  39.5 14.2 %collective-permute-start.12 = (bf16[2,4,1,128]{3,2,1,0:T(2,128)(2,1)S(1)}, bf16[2,4,1,128]{3,2,1,0:T(2,128)(2,1)S(1)}, u32[]{:S(2)}, u32[]{:S(2)}) collective-permute-start(bf16[2,4,1,128]{3,2,1,0:T(2,128)(2,1)S(1)} %get-tuple-element.40), channel_id=1, source_target_pairs={{0,1},{1,2},{2,3},{3,0},{4,5},{5,6},{6,7},{7,4},{8,9},{9,10},{10,1... | collective-permute-start | bytes 6152 | tf_op jit(solution)/shard_map/ppermute | solution.py:17
  43.0 10.8 %collective-permute-start.13 = (bf16[2,4,1,128]{3,2,1,0:T(2,128)(2,1)S(1)}, bf16[2,4,1,128]{3,2,1,0:T(2,128)(2,1)S(1)}, u32[]{:S(2)}, u32[]{:S(2)}) collective-permute-start(bf16[2,4,1,128]{3,2,1,0:T(2,128)(2,1)S(1)} %get-tuple-element.41), channel_id=1, source_target_pairs={{1,0},{2,1},{3,2},{0,3},{5,4},{6,5},{7,6},{4,7},{9,8},{10,9},{11,1... | collective-permute-start | bytes 6152 | tf_op jit(solution)/shard_map/ppermute | solution.py:20
  46.7 15.5 %collective-permute-start.16 = (bf16[2,4,1,256]{3,2,1,0:T(2,128)(2,1)S(1)}, bf16[2,4,1,256]{3,2,1,0:T(2,128)(2,1)S(1)}, u32[]{:S(2)}, u32[]{:S(2)}) collective-permute-start(bf16[2,4,1,256]{3,2,1,0:T(2,128)(2,1)S(1)} %get-tuple-element.30), channel_id=1, source_target_pairs={{0,1},{1,2},{2,3},{3,0},{4,5},{5,6},{6,7},{7,4},{8,9},{9,10},{10,1... | collective-permute-start | bytes 12296 | tf_op jit(solution)/shard_map/ppermute | solution.py:17
  49.0 13.3 %collective-permute-start.17 = (bf16[2,4,1,256]{3,2,1,0:T(2,128)(2,1)S(1)}, bf16[2,4,1,256]{3,2,1,0:T(2,128)(2,1)S(1)}, u32[]{:S(2)}, u32[]{:S(2)}) collective-permute-start(bf16[2,4,1,256]{3,2,1,0:T(2,128)(2,1)S(1)} %get-tuple-element.31), channel_id=1, source_target_pairs={{1,0},{2,1},{3,2},{0,3},{5,4},{6,5},{7,6},{4,7},{9,8},{10,9},{11,1... | collective-permute-start | bytes 12296 | tf_op jit(solution)/shard_map/ppermute | solution.py:20
  53.8 16.5 %collective-permute-start.14 = (bf16[2,1,34,128]{3,2,1,0:T(8,128)(2,1)S(1)}, bf16[2,1,34,128]{3,2,1,0:T(8,128)(2,1)S(1)}, u32[]{:S(2)}, u32[]{:S(2)}) collective-permute-start(bf16[2,1,34,128]{3,2,1,0:T(8,128)(2,1)S(1)} %get-tuple-element.39), channel_id=1, source_target_pairs={{0,4},{4,8},{8,12},{12,16},{16,20},{20,24},{24,28},{28,32},{32,36}... | collective-permute-start | bytes 52232 | tf_op jit(solution)/shard_map/ppermute | solution.py:17
  55.7 14.5 %collective-permute-start.15 = (bf16[2,1,34,128]{3,2,1,0:T(8,128)(2,1)S(1)}, bf16[2,1,34,128]{3,2,1,0:T(8,128)(2,1)S(1)}, u32[]{:S(2)}, u32[]{:S(2)}) collective-permute-start(bf16[2,1,34,128]{3,2,1,0:T(8,128)(2,1)S(1)} %get-tuple-element.38), channel_id=1, source_target_pairs={{4,0},{8,4},{12,8},{16,12},{20,16},{24,20},{28,24},{32,28},{36,32}... | collective-permute-start | bytes 52232 | tf_op jit(solution)/shard_map/ppermute | solution.py:20
  62.3 8.1 collective-permute-start.18
  64.2 7.7 collective-permute-start.19
  87.4 113.0 %all-gather.3.cloned.1.call-start = ((), (), s32[]{:S(2)}) async-start(), calls=%async_computation.3 | async-start | bytes 5898240 | tf_op jit(solution)/shard_map/all_gather | solution.py:127
  87.4 6.9 collective-permute-start.5
  92.2 6.8 collective-permute-start.4
  99.0 9.0 %collective-permute-start.6 = (bf16[2,1,34,256]{3,2,1,0:T(8,128)(2,1)S(1)}, bf16[2,1,34,256]{3,2,1,0:T(8,128)(2,1)S(1)}, u32[]{:S(2)}, u32[]{:S(2)}) collective-permute-start(bf16[2,1,34,256]{3,2,1,0:T(8,128)(2,1)S(1)} %get-tuple-element.28), channel_id=1, source_target_pairs={{4,0},{8,4},{12,8},{16,12},{20,16},{24,20},{28,24},{32,28},{36,32}... | collective-permute-start | bytes 104456 | tf_op jit(solution)/shard_map/ppermute | solution.py:20
  105.8 8.1 collective-permute-start.7
  121.6 6.1 collective-permute-start.9
  123.6 6.8 collective-permute-start.8
  130.4 6.2 collective-permute-start.10
  132.3 8.1 collective-permute-start.11
  148.9 64.8 %copy-start.1 = (bf16[589824]{0:T(1024)(128)(2,1)S(1)}, bf16[589824]{0:T(1024)(128)(2,1)}, u32[]{:S(2)}) copy-start(bf16[589824]{0:T(1024)(128)(2,1)} %all-reduce.6.cloned.1.call-done) | copy-start | bytes 3538948
  (6 other events, 70.3 us)
Sparse Core Ops, SparseCore 0:
  39.6 42.0 reduce-scatter.1
  87.5 61.3 all-reduce.5
  151.2 49.0 all-gather.2
